TPU v7x, 128 devices: a whole 4x4x4 slice. The times are simulated.
128 devices in a mesh: dp: 8 (over z_lo, x), seq: 16 (over z_hi, y, core).
Axes of the slice: x: 4, y: 4, z: 4 (z_hi: 2, z_lo: 2; z = z_hi * 2 + z_lo), core: 2. Of those that a mesh axis runs over, the one named last changes fastest.
Arguments:
- series: bfloat16 [8, 8192, 128], P('dp', 'seq'), may hold values from -6 to 6
- cotangent: bfloat16 [8, 8192, 128], P('dp', 'seq'), may hold values from -6 to 6
- w_in: bfloat16 [128, 384], replicated, may hold values from -0.5 to 0.5
- w_out: bfloat16 [128, 128], replicated, may hold values from -0.5 to 0.5
- taps: float32 [3, 384], replicated, may hold values from -3 to 3
- skip_one: float32 [128], replicated, may hold values from 0.5 to 1.5
- skip_two: float32 [128], replicated, may hold values from 0.5 to 1.5
- filter_one: float32 [8, 8192], P(None, 'seq'), may hold values from -0.0625 to 0.0625
- filter_two: float32 [8, 8192], P(None, 'seq'), may hold values from -0.0625 to 0.0625
Outputs:
- output: bfloat16 [8, 8192, 128], P('dp', 'seq')
- d_series: bfloat16 [8, 8192, 128], P('dp', 'seq')
- grad_w_in: float32 [128, 384], replicated
- grad_w_out: float32 [128, 128], replicated
- grad_taps: float32 [3, 384], replicated
- grad_skip_one: float32 [128], replicated
- grad_skip_two: float32 [128], replicated
- grad_filter_one: float32 [8, 8192], P(None, 'seq')
- grad_filter_two: float32 [8, 8192], P(None, 'seq')
All inputs are finite; a program needn't handle non-finite values.
Results may differ from a plain program's by a relative error of at most 0.015.
Values may be sent and summed in bfloat16 or wider, within the bound.
A program may use at most 128 MiB of HBM per device.

v0:
```python
import math
import jax
import jax.numpy as jnp
from jax import lax
from jax.sharding import PartitionSpec as P

FACTOR = 32


def passed_along(block, axis, distance):
    devices = range(lax.axis_size(axis))
    route = [(i - distance, i) for i in devices if i - distance in devices]
    return lax.ppermute(block, axis, route)


def grid_index(shape_pair, along):
    return lax.broadcasted_iota(jnp.int32, shape_pair, along)


def twiddle(row_index, col_index, period, direction):
    angle = (
        direction * 2.0 * math.pi / period * (row_index * col_index % period).astype(jnp.float32)
    )
    return (jnp.cos(angle), jnp.sin(angle))


def complex_mul(left_real, left_imag, right_real, right_imag):
    return (
        left_real * right_real - left_imag * right_imag,
        left_real * right_imag + left_imag * right_real,
    )


def complex_dft(real_part, imag_part, table_real, table_imag, pattern):
    highest = lax.Precision.HIGHEST
    first = jnp.einsum(pattern, table_real, real_part, precision=highest)
    second = jnp.einsum(pattern, table_imag, imag_part, precision=highest)
    third = jnp.einsum(pattern, table_real, imag_part, precision=highest)
    fourth = jnp.einsum(pattern, table_imag, real_part, precision=highest)
    return (first - second, third + fourth)


def local_dft(pieces):
    real_part, imag_part = pieces
    series_count, pair_rows, block_rows, channels = real_part.shape
    inner = block_rows // FACTOR
    real_part = real_part.reshape(series_count, pair_rows, FACTOR, inner, channels)
    imag_part = imag_part.reshape(series_count, pair_rows, FACTOR, inner, channels)
    table_real, table_imag = twiddle(
        grid_index((FACTOR, FACTOR), 0), grid_index((FACTOR, FACTOR), 1), FACTOR, -1.0
    )
    real_part, imag_part = complex_dft(
        real_part, imag_part, table_real, table_imag, "ca,erabk->ercbk"
    )
    turn_real, turn_imag = twiddle(
        grid_index((FACTOR, inner), 0), grid_index((FACTOR, inner), 1), block_rows, -1.0
    )
    real_part, imag_part = complex_mul(
        real_part, imag_part, turn_real[:, :, None], turn_imag[:, :, None]
    )
    table_real, table_imag = twiddle(
        grid_index((inner, inner), 0), grid_index((inner, inner), 1), inner, -1.0
    )
    return complex_dft(real_part, imag_part, table_real, table_imag, "db,ercbk->ercdk")


def local_inverse(real_part, imag_part):
    series_count, pair_rows, outer, inner, channels = real_part.shape
    block_rows = outer * inner
    table_real, table_imag = twiddle(
        grid_index((inner, inner), 0), grid_index((inner, inner), 1), inner, 1.0
    )
    real_part, imag_part = complex_dft(
        real_part, imag_part, table_real, table_imag, "bd,ercdk->ercbk"
    )
    turn_real, turn_imag = twiddle(
        grid_index((outer, inner), 0), grid_index((outer, inner), 1), block_rows, 1.0
    )
    real_part, imag_part = complex_mul(
        real_part, imag_part, turn_real[:, :, None], turn_imag[:, :, None]
    )
    table_real, table_imag = twiddle(
        grid_index((outer, outer), 0), grid_index((outer, outer), 1), outer, 1.0
    )
    real_part, imag_part = complex_dft(
        real_part, imag_part, table_real, table_imag, "ac,ercbk->erabk"
    )
    return (
        real_part.reshape(series_count, pair_rows, block_rows, channels),
        imag_part.reshape(series_count, pair_rows, block_rows, channels),
    )


def first_section(columns):
    highest = lax.Precision.HIGHEST
    groups = lax.axis_size("seq")
    column_width = columns.shape[2]
    period = 2 * groups * groups * column_width
    offset = lax.axis_index("seq") * column_width
    table_real, table_imag = twiddle(
        grid_index((2 * groups, groups), 0), grid_index((2 * groups, groups), 1), 2 * groups, -1.0
    )
    real_part = jnp.einsum("kn,enjc->ekjc", table_real, columns, precision=highest)
    imag_part = jnp.einsum("kn,enjc->ekjc", table_imag, columns, precision=highest)
    turn_real, turn_imag = twiddle(
        grid_index((2 * groups, column_width), 0),
        grid_index((2 * groups, column_width), 1) + offset,
        period,
        -1.0,
    )
    return complex_mul(real_part, imag_part, turn_real[:, :, None], turn_imag[:, :, None])


def last_section(pieces):
    highest = lax.Precision.HIGHEST
    part_real, part_imag = pieces
    groups = lax.axis_size("seq")
    column_width = part_real.shape[2]
    period = 2 * groups * groups * column_width
    offset = lax.axis_index("seq") * column_width
    turn_real, turn_imag = twiddle(
        grid_index((2 * groups, column_width), 0),
        grid_index((2 * groups, column_width), 1) + offset,
        period,
        1.0,
    )
    part_real, part_imag = complex_mul(
        part_real, part_imag, turn_real[:, :, None], turn_imag[:, :, None]
    )
    table_real, table_imag = twiddle(
        grid_index((groups, 2 * groups), 0), grid_index((groups, 2 * groups), 1), 2 * groups, 1.0
    )
    summed = jnp.einsum("nk,ekjc->enjc", table_real, part_real, precision=highest) - jnp.einsum(
        "nk,ekjc->enjc", table_imag, part_imag, precision=highest
    )
    return summed * (1.0 / period)


def to_frequency(real_part, imag_part):
    return local_dft(
        (
            lax.all_to_all(real_part, "seq", split_axis=1, concat_axis=2, tiled=True),
            lax.all_to_all(imag_part, "seq", split_axis=1, concat_axis=2, tiled=True),
        )
    )


def spectrum(field):
    real_part, imag_part = first_section(
        lax.all_to_all(field, "seq", split_axis=2, concat_axis=1, tiled=True)
    )
    return to_frequency(real_part, imag_part)


def signal(real_part, imag_part):
    real_part, imag_part = local_inverse(real_part, imag_part)
    columns = last_section(
        (
            lax.all_to_all(real_part, "seq", split_axis=2, concat_axis=1, tiled=True),
            lax.all_to_all(imag_part, "seq", split_axis=2, concat_axis=1, tiled=True),
        )
    )
    return lax.all_to_all(columns, "seq", split_axis=1, concat_axis=2, tiled=True)


def order_spectrum(real_part, imag_part):
    series_count, pair_rows, outer, inner, channels = real_part.shape
    block_rows = outer * inner
    real_part = jnp.swapaxes(real_part, 2, 3).reshape(series_count, pair_rows, block_rows, channels)
    imag_part = jnp.swapaxes(imag_part, 2, 3).reshape(series_count, pair_rows, block_rows, channels)
    real_part, imag_part = (
        lax.all_to_all(real_part, "seq", split_axis=2, concat_axis=1, tiled=True),
        lax.all_to_all(imag_part, "seq", split_axis=2, concat_axis=1, tiled=True),
    )
    return (jnp.swapaxes(real_part, 1, 2), jnp.swapaxes(imag_part, 1, 2))


def restore_spectrum(real_part, imag_part):
    real_part = jnp.swapaxes(real_part, 1, 2)
    imag_part = jnp.swapaxes(imag_part, 1, 2)
    real_part, imag_part = (
        lax.all_to_all(real_part, "seq", split_axis=1, concat_axis=2, tiled=True),
        lax.all_to_all(imag_part, "seq", split_axis=1, concat_axis=2, tiled=True),
    )
    series_count, pair_rows, block_rows, channels = real_part.shape
    inner = block_rows // FACTOR
    real_part = jnp.swapaxes(
        real_part.reshape(series_count, pair_rows, inner, FACTOR, channels), 2, 3
    )
    imag_part = jnp.swapaxes(
        imag_part.reshape(series_count, pair_rows, inner, FACTOR, channels), 2, 3
    )
    return (real_part, imag_part)


def transform(field):
    real_part, imag_part = spectrum(field)
    real_part, imag_part = order_spectrum(real_part, imag_part)
    return (real_part, imag_part)


def untransform(real_part, imag_part, in_columns):
    real_part, imag_part = restore_spectrum(real_part, imag_part)
    return signal(real_part, imag_part)


def widen_groups(pieces, channels):
    real_part, imag_part = pieces
    repeat_count = channels // real_part.shape[-1]
    return (
        jnp.repeat(real_part, repeat_count, axis=-1),
        jnp.repeat(imag_part, repeat_count, axis=-1),
    )


def group_sum(pieces, filters):
    result = []
    for piece in pieces:
        channels = piece.shape[-1]
        reshaped = piece.reshape(piece.shape[:-1] + (filters, channels // filters))
        result.append(jnp.sum(jnp.sum(reshaped, axis=-1), axis=0, keepdims=True))
    return (result[0], result[1])


def rows_before(field):
    return passed_along(field[:, :, -2:], "seq", 1)


def rows_after(field):
    return passed_along(field[:, :, :2], "seq", -1)


def filter_blocks(filter_rows):
    return filter_rows.T.reshape(1, 1, filter_rows.shape[1], filter_rows.shape[0])


def shards(series, cotangent, w_in, w_out, taps, skip_one, skip_two, filter_one, filter_two):
    series_count, block_rows, width_d = series.shape
    filters = filter_one.shape[0]
    token_total = series_count * lax.axis_size("dp") * block_rows * lax.axis_size("seq")
    grad_scale = 1.0 / math.sqrt(token_total)
    series_four = series.reshape(series_count, 1, block_rows, width_d)
    cot_four = cotangent.reshape(series_count, 1, block_rows, width_d)
    series_here, cot_here = (series_four, cot_four)
    projected = jnp.einsum("entd,dc->entc", series_here, w_in, preferred_element_type=jnp.float32)
    before = rows_before(projected)
    extended = jnp.concatenate([before, projected], axis=2)
    run_rows = projected.shape[2]
    convolved = (
        taps[0] * extended[:, :, 2:]
        + taps[1] * extended[:, :, 1:-1]
        + taps[2] * extended[:, :, :-2]
    )
    value_part = convolved[..., :width_d]
    gate_one = convolved[..., width_d : 2 * width_d]
    gate_two = convolved[..., 2 * width_d :]
    spec_one = transform(filter_blocks(filter_one))
    spec_two = transform(filter_blocks(filter_two))
    one_real, one_imag = widen_groups(spec_one, width_d)
    two_real, two_imag = widen_groups(spec_two, width_d)
    value_real, value_imag = transform(value_part)
    y_one = (
        untransform(*complex_mul(one_real, one_imag, value_real, value_imag), False)
        + skip_one * value_part
    )
    gated_mid = gate_one * y_one
    mid_real, mid_imag = transform(gated_mid)
    y_two = (
        untransform(*complex_mul(two_real, two_imag, mid_real, mid_imag), False)
        + skip_two * gated_mid
    )
    product = (gate_two * y_two).astype(jnp.bfloat16)
    output = jnp.einsum("entc,cd->entd", product, w_out, preferred_element_type=jnp.float32).astype(
        jnp.bfloat16
    )
    d_product = jnp.einsum("entd,cd->entc", cot_here, w_out, preferred_element_type=jnp.float32)
    grad_two = d_product * gate_two
    d_gate_two = d_product * y_two
    gtwo_real, gtwo_imag = transform(grad_two)
    d_mid = (
        untransform(*complex_mul(two_real, -two_imag, gtwo_real, gtwo_imag), False)
        + skip_two * grad_two
    )
    filter_two_spec = group_sum(complex_mul(mid_real, -mid_imag, gtwo_real, gtwo_imag), filters)
    filter_two_time = untransform(filter_two_spec[0], filter_two_spec[1], False)[0, 0].T
    grad_one = d_mid * gate_one
    d_gate_one = d_mid * y_one
    gone_real, gone_imag = transform(grad_one)
    d_value = (
        untransform(*complex_mul(one_real, -one_imag, gone_real, gone_imag), False)
        + skip_one * grad_one
    )
    filter_one_spec = group_sum(complex_mul(value_real, -value_imag, gone_real, gone_imag), filters)
    filter_one_time = untransform(filter_one_spec[0], filter_one_spec[1], False)[0, 0].T
    d_convolved = jnp.concatenate([d_value, d_gate_one, d_gate_two], axis=3)
    after = rows_after(d_convolved)
    extended_back = jnp.concatenate([d_convolved, after], axis=2)
    d_projected = (
        taps[0] * extended_back[:, :, :-2]
        + taps[1] * extended_back[:, :, 1:-1]
        + taps[2] * extended_back[:, :, 2:]
    ).astype(jnp.bfloat16)
    d_series = jnp.einsum(
        "entc,dc->entd", d_projected, w_in, preferred_element_type=jnp.float32
    ).astype(jnp.bfloat16)
    local_w_in = jnp.einsum(
        "entd,entc->dc", series_here, d_projected, preferred_element_type=jnp.float32
    )
    local_w_out = jnp.einsum("entc,entd->cd", product, cot_here, preferred_element_type=jnp.float32)
    local_taps = jnp.stack(
        [
            jnp.sum(
                d_convolved * extended[:, :, 2 - offset : 2 - offset + run_rows], axis=(0, 1, 2)
            )
            for offset in range(3)
        ]
    )
    local_skip_one = jnp.sum(grad_one * value_part, axis=(0, 1, 2))
    local_skip_two = jnp.sum(grad_two * gated_mid, axis=(0, 1, 2))
    grad_w_in, grad_w_out, grad_taps, grad_skip_one, grad_skip_two = lax.psum(
        (local_w_in, local_w_out, local_taps, local_skip_one, local_skip_two), ("dp", "seq")
    )
    grad_filter_one, grad_filter_two = (
        lax.psum(filter_one_time.astype(jnp.bfloat16), "dp").astype(jnp.float32),
        lax.psum(filter_two_time.astype(jnp.bfloat16), "dp").astype(jnp.float32),
    )
    output = output.reshape(series_count, block_rows, width_d)
    d_series = d_series.reshape(series_count, block_rows, width_d)
    return (
        output,
        d_series,
        grad_scale * grad_w_in,
        grad_scale * grad_w_out,
        grad_scale * grad_taps,
        grad_scale * grad_skip_one,
        grad_scale * grad_skip_two,
        grad_scale * grad_filter_one,
        grad_scale * grad_filter_two,
    )


def solution(mesh):
    in_specs = (
        P("dp", "seq", None),
        P("dp", "seq", None),
        P(),
        P(),
        P(),
        P(),
        P(),
        P(None, "seq"),
        P(None, "seq"),
    )
    out_specs = (
        P("dp", "seq", None),
        P("dp", "seq", None),
        P(),
        P(),
        P(),
        P(),
        P(),
        P(None, "seq"),
        P(None, "seq"),
    )
    return jax.shard_map(shards, mesh=mesh, in_specs=in_specs, out_specs=out_specs, check_vma=False)
```

profile of v0, /device:TPU:1, one launch (start us, length us, event | category | flops | bytes accessed | tf_op | source)
XLA Modules:
  0.0 1293.6 jit_solution(11738205178397126315)
XLA Ops:
  10.7 9.3 all-to-all-start.4
  28.0 6.5 all-to-all-start
  36.5 5.3 all-to-all-done
  50.9 5.5 all-to-all-done.6
  61.6 5.8 all-to-all-done.5
  73.3 6.6 all-to-all-done.8
  89.2 9.1 all-to-all-done.9
  107.8 6.7 all-to-all-done.10
  132.7 5.1 all-to-all-done.12
  144.8 8.3 all-to-all-done.11
  163.8 5.5 all-to-all-done.13
  188.9 8.4 all-to-all-done.14
  207.4 6.5 all-to-all-done.15
  222.0 5.6 all-to-all-start.16
  231.7 7.3 all-to-all-done.16
  245.4 9.6 all-to-all-done.17
  263.8 7.9 all-to-all-done.18
  283.9 12.2 all_to_all.876
  316.0 7.3 all-to-all-start.2
  330.7 6.4 all-to-all-start.31
  348.5 5.3 all-to-all-start.32
  368.1 7.2 all-to-all-start.21
  379.5 7.3 all-to-all-done.21
  386.8 5.0 all-to-all-start.20
  398.3 5.1 all-to-all-done.20
  403.4 5.3 all-to-all-start.3
  417.1 7.3 all-to-all-start.23
  441.4 6.3 all-to-all-done.33
  447.7 5.0 all-to-all-start.34
  457.0 7.4 all-to-all-done.34
  464.3 5.6 all-to-all-start.24
  474.2 7.2 all-to-all-done.24
  481.4 5.1 all-to-all-start.22
  516.8 10.7 fusion.14
  530.6 7.3 all-to-all-start.26
  540.9 8.3 all-to-all-done.26
  549.3 5.0 all-to-all-start.25
  557.4 8.5 all-to-all-done.25
  565.9 5.3 all-to-all-start.36
  592.7 6.0 all-to-all-done.35
  609.3 5.4 all-to-all-start.37
  619.8 6.3 all-to-all-done.37
  626.1 5.1 all-to-all-start.38
  635.3 7.5 all-to-all-done.38
  651.9 7.5 all-to-all-done.28
  669.6 5.7 all-to-all-done.27
  687.6 6.3 all-to-all-done.39
  693.9 12.0 all_to_all.877
  708.8 5.1 all-to-all-start.40
  725.9 7.3 all-to-all-start.56
  762.5 5.9 all-to-all-done.41
  792.6 6.8 all-to-all-start.43
  835.4 8.3 fusion.12
  874.4 7.4 all-to-all-start.57
  933.1 7.3 all-to-all-start.46
  945.0 6.7 all-to-all-done.46
  958.3 9.3 all-to-all-done.45
  967.7 5.4 all-to-all-start.59
  998.8 8.4 all-to-all-done.47
  1015.1 27.4 %all-reduce.2 = (bf16[8,512]{1,0:T(8,128)(2,1)}, bf16[8,512]{1,0:T(8,128)(2,1)}) all-reduce(bf16[8,512]{1,0:T(8,128)(2,1)S(1)} %bitcast.1449, bf16[8,512]{1,0:T(8,128)(2,1)S(1)} %bitcast.1448), channel_id=1, replica_groups=mesh['dp'=8,'seq'=16] {'dp'}, use_global_device_ids=true, to_apply=%region_12.13 | all-reduce | flops 8192 | bytes 32768 | tf_op jit(solution)/shard_map/psum | solution.py:324
  1046.1 14.8 %all-to-all-start.49 = ((f32[1,16,32,128]{3,2,0,1:T(8,128)}), f32[1,16,32,128]{3,2,0,1:T(8,128)S(1)}, u32[]{:S(2)}, u32[]{:S(2)}) async-start(f32[1,16,32,128]{3,2,0,1:T(8,128)} %copy.829), calls=%async_computation.49 | async-start | bytes 524288 | tf_op jit(solution)/shard_map/all_to_all | solution.py:163
  1062.2 7.4 all-to-all-done.49
  1075.5 66.5 %all-reduce = (f32[3,384]{1,0:T(4,128)S(1)}, f32[128]{0:T(128)S(1)}, f32[128]{0:T(128)S(1)}) all-reduce(f32[3,384]{1,0:T(4,128)S(1)} %pad_maximum_fusion.3, f32[128]{0:T(128)S(1)} %copy-done.70, f32[128]{0:T(128)S(1)} %copy-done.69), channel_id=1, replica_groups=mesh['dp'=8,'seq'=16] {'dp','seq'}, use_global_device_ids=true, to_apply=%region_5.6 | all-reduce | flops 1408 | bytes 11264 | tf_op jit(solution)/shard_map/psum | solution.py:320
  1145.6 137.8 %all-reduce.5.cloned.1.call-done = (f32[128,384]{0,1:T(8,128)}, f32[128,128]{1,0:T(8,128)}) async-done(((f32[128,384]{0,1:T(8,128)}, f32[128,128]{1,0:T(8,128)}), (f32[128,384]{0,1:T(8,128)}, f32[128,128]{1,0:T(8,128)})) %all-reduce.5.cloned.1.call-update) | async-done | bytes 262160 | tf_op jit(solution)/shard_map/psum | solution.py:320
  (588 shorter events, 614.5 us)
Async XLA Ops:
  10.7 17.3 %all-to-all-start.4 = ((f32[16,1,256]{2,1,0:T(1,128)}), f32[16,1,256]{2,1,0:T(1,128)S(1)}, u32[]{:S(2)}, u32[]{:S(2)}) async-start(f32[16,1,256]{2,1,0:T(1,128)} %reshape.1187), calls=%async_computation.4 | async-start | bytes 32768 | tf_op jit(solution)/shard_map/all_to_all | solution.py:150
  21.2 27.8 %collective-permute-start = (f32[1,1,2,384]{3,2,1,0:T(2,128)S(1)}, f32[1,1,2,384]{3,2,1,0:T(2,128)S(1)}, u32[]{:S(2)}, u32[]{:S(2)}) collective-permute-start(f32[1,1,2,384]{3,2,1,0:T(2,128)S(1)} %slice.53), channel_id=1, source_target_pairs={{0,1},{1,2},{2,3},{3,4},{4,5},{5,6},{6,7},{7,8},{8,9},{9,10},{10,1... | collective-permute-start | bytes 9224 | tf_op jit(solution)/shard_map/ppermute | solution.py:13
  25.7 54.9 %copy-start.47 = (f32[32,32]{0,1:T(8,128)}, f32[32,32]{0,1:T(8,128)S(1)}, u32[]{:S(2)}) copy-start(f32[32,32]{0,1:T(8,128)S(1)} %copy.646) | copy-start | bytes 12292
  25.8 54.9 %copy-start.48 = (f32[32,32]{0,1:T(8,128)}, f32[32,32]{0,1:T(8,128)S(1)}, u32[]{:S(2)}) copy-start(f32[32,32]{0,1:T(8,128)S(1)} %copy.644) | copy-start | bytes 12292
  28.0 13.8 %all-to-all-start = ((f32[16,1,256]{2,1,0:T(1,128)}), f32[16,1,256]{2,1,0:T(1,128)S(1)}, u32[]{:S(2)}, u32[]{:S(2)}) async-start(f32[16,1,256]{2,1,0:T(1,128)} %reshape.1197), calls=%async_computation | async-start | bytes 32768 | tf_op jit(solution)/shard_map/all_to_all | solution.py:150
  45.3 11.1 all-to-all-start.6
  56.4 11.1 all-to-all-start.5
  67.4 12.5 all-to-all-start.8
  82.6 15.7 %all-to-all-start.9 = ((f32[1,32,32,128]{3,2,0,1:T(8,128)}), f32[1,32,32,128]{3,2,0,1:T(8,128)S(1)}, u32[]{:S(2)}, u32[]{:S(2)}) async-start(f32[1,32,32,128]{3,2,0,1:T(8,128)} %copy.647), calls=%async_computation.9 | async-start | bytes 1048576 | tf_op jit(solution)/shard_map/all_to_all | solution.py:142
  98.3 16.1 %all-to-all-start.10 = ((f32[1,32,32,128]{3,2,0,1:T(8,128)}), f32[1,32,32,128]{3,2,0,1:T(8,128)S(1)}, u32[]{:S(2)}, u32[]{:S(2)}) async-start(f32[1,32,32,128]{3,2,0,1:T(8,128)} %copy.650), calls=%async_computation.10 | async-start | bytes 1048576 | tf_op jit(solution)/shard_map/all_to_all | solution.py:143
  114.4 12.3 all-to-all-start.7
  126.7 11.1 all-to-all-start.12
  137.8 15.2 %all-to-all-start.11 = ((f32[1,2,512,128]{3,1,0,2:T(2,128)}), f32[1,2,512,128]{3,1,0,2:T(2,128)S(1)}, u32[]{:S(2)}, u32[]{:S(2)}) async-start(f32[1,2,512,128]{3,1,0,2:T(2,128)} %copy.658), calls=%async_computation.11 | async-start | bytes 1048576 | tf_op jit(solution)/shard_map/all_to_all | solution.py:172
  153.0 16.2 %all-to-all-start.13 = ((f32[1,2,512,128]{3,1,0,2:T(2,128)}), f32[1,2,512,128]{3,1,0,2:T(2,128)S(1)}, u32[]{:S(2)}, u32[]{:S(2)}) async-start(f32[1,2,512,128]{3,1,0,2:T(2,128)} %copy.669), calls=%async_computation.13 | async-start | bytes 1048576 | tf_op jit(solution)/shard_map/all_to_all | solution.py:173
  181.4 15.9 %all-to-all-start.14 = ((f32[1,32,32,128]{3,2,0,1:T(8,128)}), f32[1,32,32,128]{3,2,0,1:T(8,128)S(1)}, u32[]{:S(2)}, u32[]{:S(2)}) async-start(f32[1,32,32,128]{3,2,0,1:T(8,128)} %copy.673), calls=%async_computation.14 | async-start | bytes 1048576 | tf_op jit(solution)/shard_map/all_to_all | solution.py:182
  197.3 16.6 %all-to-all-start.15 = ((f32[1,32,32,128]{3,2,0,1:T(8,128)}), f32[1,32,32,128]{3,2,0,1:T(8,128)}, u32[]{:S(2)}, u32[]{:S(2)}) async-start(f32[1,32,32,128]{3,2,0,1:T(8,128)} %copy.675), calls=%async_computation.15 | async-start | bytes 1048576 | tf_op jit(solution)/shard_map/all_to_all | solution.py:183
  222.0 17.0 %all-to-all-start.16 = ((f32[1,2,512,128]{3,1,0,2:T(2,128)}), f32[1,2,512,128]{3,1,0,2:T(2,128)}, u32[]{:S(2)}, u32[]{:S(2)}) async-start(f32[1,2,512,128]{3,1,0,2:T(2,128)} %copy.682), calls=%async_computation.16 | async-start | bytes 1048576 | tf_op jit(solution)/shard_map/all_to_all | solution.py:159
  239.0 15.9 %all-to-all-start.17 = ((f32[1,2,512,128]{3,1,0,2:T(2,128)}), f32[1,2,512,128]{3,1,0,2:T(2,128)S(1)}, u32[]{:S(2)}, u32[]{:S(2)}) async-start(f32[1,2,512,128]{3,1,0,2:T(2,128)} %copy.688), calls=%async_computation.17 | async-start | bytes 1048576 | tf_op jit(solution)/shard_map/all_to_all | solution.py:160
  258.6 13.1 %all-to-all-start.18 = ((f32[1,16,32,128]{3,2,0,1:T(8,128)}), f32[1,16,32,128]{3,2,0,1:T(8,128)S(1)}, u32[]{:S(2)}, u32[]{:S(2)}) async-start(f32[1,16,32,128]{3,2,0,1:T(8,128)} %copy.693), calls=%async_computation.18 | async-start | bytes 524288 | tf_op jit(solution)/shard_map/all_to_all | solution.py:163
  271.7 12.2 all-to-all-start.1
  296.1 19.9 %all-to-all-start.30 = ((f32[1,1,512,128]{3,1,0,2:T(1,128)}), f32[1,1,512,128]{3,1,0,2:T(1,128)}, u32[]{:S(2)}, u32[]{:S(2)}) async-start(f32[1,1,512,128]{3,1,0,2:T(1,128)} %bitcast.259), calls=%async_computation.30 | async-start | bytes 524288 | tf_op jit(solution)/shard_map/all_to_all | solution.py:150
  316.0 14.7 %all-to-all-start.2 = ((f32[16,1,512]{2,1,0:T(1,128)}), f32[16,1,512]{2,1,0:T(1,128)}, u32[]{:S(2)}, u32[]{:S(2)}) async-start(f32[16,1,512]{2,1,0:T(1,128)} %reshape.1199), calls=%async_computation.2 | async-start | bytes 65536 | tf_op jit(solution)/shard_map/all_to_all | solution.py:143
  330.7 17.8 %all-to-all-start.31 = ((f32[1,32,32,128]{3,2,0,1:T(8,128)}), f32[1,32,32,128]{3,2,0,1:T(8,128)}, u32[]{:S(2)}, u32[]{:S(2)}) async-start(f32[1,32,32,128]{3,2,0,1:T(8,128)} %copy.745), calls=%async_computation.31 | async-start | bytes 1048576 | tf_op jit(solution)/shard_map/all_to_all | solution.py:142
  348.5 19.5 %all-to-all-start.32 = ((f32[1,32,32,128]{3,2,0,1:T(8,128)}), f32[1,32,32,128]{3,2,0,1:T(8,128)}, u32[]{:S(2)}, u32[]{:S(2)}) async-start(f32[1,32,32,128]{3,2,0,1:T(8,128)} %copy.748), calls=%async_computation.32 | async-start | bytes 1048576 | tf_op jit(solution)/shard_map/all_to_all | solution.py:143
  368.1 18.7 %all-to-all-start.21 = ((f32[1,32,32,128]{3,2,0,1:T(8,128)}), f32[1,32,32,128]{3,2,0,1:T(8,128)}, u32[]{:S(2)}, u32[]{:S(2)}) async-start(f32[1,32,32,128]{3,2,0,1:T(8,128)} %copy.700), calls=%async_computation.21 | async-start | bytes 1048576 | tf_op jit(solution)/shard_map/all_to_all | solution.py:143
  386.8 16.6 %all-to-all-start.20 = ((f32[1,32,32,128]{3,2,0,1:T(8,128)}), f32[1,32,32,128]{3,2,0,1:T(8,128)}, u32[]{:S(2)}, u32[]{:S(2)}) async-start(f32[1,32,32,128]{3,2,0,1:T(8,128)} %copy.697), calls=%async_computation.20 | async-start | bytes 1048576 | tf_op jit(solution)/shard_map/all_to_all | solution.py:142
  403.4 13.7 %all-to-all-start.3 = ((f32[16,1,512]{2,1,0:T(1,128)}), f32[16,1,512]{2,1,0:T(1,128)}, u32[]{:S(2)}, u32[]{:S(2)}) async-start(f32[16,1,512]{2,1,0:T(1,128)} %reshape.1205), calls=%async_computation.3 | async-start | bytes 65536 | tf_op jit(solution)/shard_map/all_to_all | solution.py:172
  417.1 14.7 %all-to-all-start.23 = ((f32[16,1,512]{2,1,0:T(1,128)}), f32[16,1,512]{2,1,0:T(1,128)}, u32[]{:S(2)}, u32[]{:S(2)}) async-start(f32[16,1,512]{2,1,0:T(1,128)} %reshape.1203), calls=%async_computation.23 | async-start | bytes 65536 | tf_op jit(solution)/shard_map/all_to_all | solution.py:173
  431.8 15.9 %all-to-all-start.33 = ((f32[1,2,512,128]{3,1,0,2:T(2,128)}), f32[1,2,512,128]{3,1,0,2:T(2,128)}, u32[]{:S(2)}, u32[]{:S(2)}) async-start(f32[1,2,512,128]{3,1,0,2:T(2,128)} %copy.756), calls=%async_computation.33 | async-start | bytes 1048576 | tf_op jit(solution)/shard_map/all_to_all | solution.py:172
  447.7 16.6 %all-to-all-start.34 = ((f32[1,2,512,128]{3,1,0,2:T(2,128)}), f32[1,2,512,128]{3,1,0,2:T(2,128)}, u32[]{:S(2)}, u32[]{:S(2)}) async-start(f32[1,2,512,128]{3,1,0,2:T(2,128)} %copy.763), calls=%async_computation.34 | async-start | bytes 1048576 | tf_op jit(solution)/shard_map/all_to_all | solution.py:173
  464.3 17.0 %all-to-all-start.24 = ((f32[1,2,512,128]{3,1,0,2:T(2,128)}), f32[1,2,512,128]{3,1,0,2:T(2,128)}, u32[]{:S(2)}, u32[]{:S(2)}) async-start(f32[1,2,512,128]{3,1,0,2:T(2,128)} %copy.719), calls=%async_computation.24 | async-start | bytes 1048576 | tf_op jit(solution)/shard_map/all_to_all | solution.py:173
  481.4 22.5 %all-to-all-start.22 = ((f32[1,2,512,128]{3,1,0,2:T(2,128)}), f32[1,2,512,128]{3,1,0,2:T(2,128)}, u32[]{:S(2)}, u32[]{:S(2)}) async-start(f32[1,2,512,128]{3,1,0,2:T(2,128)} %copy.708), calls=%async_computation.22 | async-start | bytes 1048576 | tf_op jit(solution)/shard_map/all_to_all | solution.py:172
  530.6 18.7 %all-to-all-start.26 = ((f32[1,32,32,128]{3,2,0,1:T(8,128)}), f32[1,32,32,128]{3,2,0,1:T(8,128)S(1)}, u32[]{:S(2)}, u32[]{:S(2)}) async-start(f32[1,32,32,128]{3,2,0,1:T(8,128)} %copy.725), calls=%async_computation.26 | async-start | bytes 1048576 | tf_op jit(solution)/shard_map/all_to_all | solution.py:183
  549.3 16.6 %all-to-all-start.25 = ((f32[1,32,32,128]{3,2,0,1:T(8,128)}), f32[1,32,32,128]{3,2,0,1:T(8,128)}, u32[]{:S(2)}, u32[]{:S(2)}) async-start(f32[1,32,32,128]{3,2,0,1:T(8,128)} %copy.723), calls=%async_computation.25 | async-start | bytes 1048576 | tf_op jit(solution)/shard_map/all_to_all | solution.py:182
  565.9 16.8 %all-to-all-start.36 = ((f32[1,32,32,128]{3,2,0,1:T(8,128)}), f32[1,32,32,128]{3,2,0,1:T(8,128)}, u32[]{:S(2)}, u32[]{:S(2)}) async-start(f32[1,32,32,128]{3,2,0,1:T(8,128)} %copy.769), calls=%async_computation.36 | async-start | bytes 1048576 | tf_op jit(solution)/shard_map/all_to_all | solution.py:183
  582.7 15.9 %all-to-all-start.35 = ((f32[1,32,32,128]{3,2,0,1:T(8,128)}), f32[1,32,32,128]{3,2,0,1:T(8,128)S(1)}, u32[]{:S(2)}, u32[]{:S(2)}) async-start(f32[1,32,32,128]{3,2,0,1:T(8,128)} %copy.767), calls=%async_computation.35 | async-start | bytes 1048576 | tf_op jit(solution)/shard_map/all_to_all | solution.py:182
  609.3 16.8 %all-to-all-start.37 = ((f32[1,2,512,128]{3,1,0,2:T(2,128)}), f32[1,2,512,128]{3,1,0,2:T(2,128)}, u32[]{:S(2)}, u32[]{:S(2)}) async-start(f32[1,2,512,128]{3,1,0,2:T(2,128)} %copy.774), calls=%async_computation.37 | async-start | bytes 1048576 | tf_op jit(solution)/shard_map/all_to_all | solution.py:159
  626.1 16.6 %all-to-all-start.38 = ((f32[1,2,512,128]{3,1,0,2:T(2,128)}), f32[1,2,512,128]{3,1,0,2:T(2,128)}, u32[]{:S(2)}, u32[]{:S(2)}) async-start(f32[1,2,512,128]{3,1,0,2:T(2,128)} %copy.780), calls=%async_computation.38 | async-start | bytes 1048576 | tf_op jit(solution)/shard_map/all_to_all | solution.py:160
  642.7 16.6 %all-to-all-start.28 = ((f32[1,2,512,128]{3,1,0,2:T(2,128)}), f32[1,2,512,128]{3,1,0,2:T(2,128)}, u32[]{:S(2)}, u32[]{:S(2)}) async-start(f32[1,2,512,128]{3,1,0,2:T(2,128)} %copy.736), calls=%async_computation.28 | async-start | bytes 1048576 | tf_op jit(solution)/shard_map/all_to_all | solution.py:160
  659.4 15.9 %all-to-all-start.27 = ((f32[1,2,512,128]{3,1,0,2:T(2,128)}), f32[1,2,512,128]{3,1,0,2:T(2,128)S(1)}, u32[]{:S(2)}, u32[]{:S(2)}) async-start(f32[1,2,512,128]{3,1,0,2:T(2,128)} %copy.730), calls=%async_computation.27 | async-start | bytes 1048576 | tf_op jit(solution)/shard_map/all_to_all | solution.py:159
  680.0 13.8 %all-to-all-start.39 = ((f32[1,16,32,128]{3,2,0,1:T(8,128)}), f32[1,16,32,128]{3,2,0,1:T(8,128)}, u32[]{:S(2)}, u32[]{:S(2)}) async-start(f32[1,16,32,128]{3,2,0,1:T(8,128)} %copy.785), calls=%async_computation.39 | async-start | bytes 524288 | tf_op jit(solution)/shard_map/all_to_all | solution.py:163
  708.8 17.2 %all-to-all-start.40 = ((f32[1,1,512,128]{3,1,0,2:T(1,128)}), f32[1,1,512,128]{3,1,0,2:T(1,128)}, u32[]{:S(2)}, u32[]{:S(2)}) async-start(f32[1,1,512,128]{3,1,0,2:T(1,128)} %bitcast.1339), calls=%async_computation.40 | async-start | bytes 524288 | tf_op jit(solution)/shard_map/all_to_all | solution.py:150
  725.9 14.7 %all-to-all-start.56 = ((f32[16,1,512]{2,1,0:T(1,128)}), f32[16,1,512]{2,1,0:T(1,128)}, u32[]{:S(2)}, u32[]{:S(2)}) async-start(f32[16,1,512]{2,1,0:T(1,128)} %reshape.1217), calls=%async_computation.56 | async-start | bytes 65536 | tf_op jit(solution)/shard_map/all_to_all | solution.py:183
  740.6 11.7 all-to-all-start.55
  752.4 15.9 %all-to-all-start.41 = ((f32[1,32,32,128]{3,2,0,1:T(8,128)}), f32[1,32,32,128]{3,2,0,1:T(8,128)}, u32[]{:S(2)}, u32[]{:S(2)}) async-start(f32[1,32,32,128]{3,2,0,1:T(8,128)} %copy.789), calls=%async_computation.41 | async-start | bytes 1048576 | tf_op jit(solution)/shard_map/all_to_all | solution.py:142
  768.3 16.6 %all-to-all-start.42 = ((f32[1,32,32,128]{3,2,0,1:T(8,128)}), f32[1,32,32,128]{3,2,0,1:T(8,128)}, u32[]{:S(2)}, u32[]{:S(2)}) async-start(f32[1,32,32,128]{3,2,0,1:T(8,128)} %copy.792), calls=%async_computation.42 | async-start | bytes 1048576 | tf_op jit(solution)/shard_map/all_to_all | solution.py:143
  792.6 18.3 %all-to-all-start.43 = ((f32[1,2,512,128]{3,1,0,2:T(2,128)}), f32[1,2,512,128]{3,1,0,2:T(2,128)}, u32[]{:S(2)}, u32[]{:S(2)}) async-start(f32[1,2,512,128]{3,1,0,2:T(2,128)} %copy.800), calls=%async_computation.43 | async-start | bytes 1048576 | tf_op jit(solution)/shard_map/all_to_all | solution.py:172
  810.9 16.6 %all-to-all-start.44 = ((f32[1,2,512,128]{3,1,0,2:T(2,128)}), f32[1,2,512,128]{3,1,0,2:T(2,128)}, u32[]{:S(2)}, u32[]{:S(2)}) async-start(f32[1,2,512,128]{3,1,0,2:T(2,128)} %copy.807), calls=%async_computation.44 | async-start | bytes 1048576 | tf_op jit(solution)/shard_map/all_to_all | solution.py:173
  849.9 12.4 all-to-all-start.50
  862.2 12.1 all-to-all-start.51
  874.4 14.6 %all-to-all-start.57 = ((f32[16,1,512]{2,1,0:T(1,128)}), f32[16,1,512]{2,1,0:T(1,128)S(1)}, u32[]{:S(2)}, u32[]{:S(2)}) async-start(f32[16,1,512]{2,1,0:T(1,128)} %reshape.1223), calls=%async_computation.57 | async-start | bytes 65536 | tf_op jit(solution)/shard_map/all_to_all | solution.py:159
  889.0 11.1 all-to-all-start.58
  900.0 11.1 all-to-all-start.53
  911.1 21.9 %all-to-all-start.52 = ((f32[16,1,512]{2,1,0:T(1,128)}), f32[16,1,512]{2,1,0:T(1,128)}, u32[]{:S(2)}, u32[]{:S(2)}) async-start(f32[16,1,512]{2,1,0:T(1,128)} %reshape.1213), calls=%async_computation.52 | async-start | bytes 65536 | tf_op jit(solution)/shard_map/all_to_all | solution.py:159
  933.1 18.7 %all-to-all-start.46 = ((f32[1,32,32,128]{3,2,0,1:T(8,128)}), f32[1,32,32,128]{3,2,0,1:T(8,128)S(1)}, u32[]{:S(2)}, u32[]{:S(2)}) async-start(f32[1,32,32,128]{3,2,0,1:T(8,128)} %copy.813), calls=%async_computation.46 | async-start | bytes 1048576 | tf_op jit(solution)/shard_map/all_to_all | solution.py:183
  951.8 15.9 %all-to-all-start.45 = ((f32[1,32,32,128]{3,2,0,1:T(8,128)}), f32[1,32,32,128]{3,2,0,1:T(8,128)S(1)}, u32[]{:S(2)}, u32[]{:S(2)}) async-start(f32[1,32,32,128]{3,2,0,1:T(8,128)} %copy.811), calls=%async_computation.45 | async-start | bytes 1048576 | tf_op jit(solution)/shard_map/all_to_all | solution.py:182
  967.7 12.4 all-to-all-start.59
  980.1 11.7 all-to-all-start.54
  991.8 15.4 %all-to-all-start.47 = ((f32[1,2,512,128]{3,1,0,2:T(2,128)}), f32[1,2,512,128]{3,1,0,2:T(2,128)S(1)}, u32[]{:S(2)}, u32[]{:S(2)}) async-start(f32[1,2,512,128]{3,1,0,2:T(2,128)} %copy.818), calls=%async_computation.47 | async-start | bytes 1048576 | tf_op jit(solution)/shard_map/all_to_all | solution.py:159
  1007.2 35.4 %all-to-all-start.48 = ((f32[1,2,512,128]{3,1,0,2:T(2,128)}), f32[1,2,512,128]{3,1,0,2:T(2,128)S(1)}, u32[]{:S(2)}, u32[]{:S(2)}) async-start(f32[1,2,512,128]{3,1,0,2:T(2,128)} %copy.824), calls=%async_computation.48 | async-start | bytes 1048576 | tf_op jit(solution)/shard_map/all_to_all | solution.py:160
  1046.1 23.5 %all-to-all-start.49 = ((f32[1,16,32,128]{3,2,0,1:T(8,128)}), f32[1,16,32,128]{3,2,0,1:T(8,128)S(1)}, u32[]{:S(2)}, u32[]{:S(2)}) async-start(f32[1,16,32,128]{3,2,0,1:T(8,128)} %copy.829), calls=%async_computation.49 | async-start | bytes 524288 | tf_op jit(solution)/shard_map/all_to_all | solution.py:163
  1060.9 222.4 %all-reduce.5.cloned.1.call-start = ((), (), s32[]{:S(2)}) async-start(), calls=%async_computation.60 | async-start | bytes 524288 | tf_op jit(solution)/shard_map/psum | solution.py:320
  1069.8 4.9 collective-permute-start.1
  1074.8 69.8 %copy-start.46 = (bf16[128,384]{1,0:T(8,128)(2,1)S(1)}, bf16[128,384]{1,0:T(8,128)(2,1)}, u32[]{:S(2)}) copy-start(bf16[128,384]{1,0:T(8,128)(2,1)} %param.11) | copy-start | bytes 294916
  (68 other events, 636.6 us)
Sparse Core Ops, SparseCore 0:
  1144.8 138.5 all-reduce.4
where the time goes:
time: 1310 us; the launch traced here: 1290 us
  waiting for transfers between devices  427 us (33%)
  starting transfers between devices  315 us (24%)
  local copies, waits for them, and re-layouts  193 us (15%)
  matrix products  149 us (11%)
  blocking collectives  118 us (9%)
  other arithmetic  75 us (6%)
  between operations  16.5 us (1%)
    psum x1, waiting for transfers between devices, shards(): lax.psum((local_w_in, local_w_out, local_taps, local_skip_one, local_skip...  138 us
    psum x1, blocking collectives, shards(): lax.psum((local_w_in, local_w_out, local_taps, local_skip_one, local_skip...  66.5 us
    unnamed x186, local copies, waits for them, and re-layouts  50.7 us
    all_to_all x6, waiting for transfers between devices, restore_spectrum(): lax.all_to_all(real_part, 'seq', split_axis=1, concat_axis=2, tiled=True)  38.3 us
    all_to_all x6, starting transfers between devices, restore_spectrum(): lax.all_to_all(imag_part, 'seq', split_axis=1, concat_axis=2, tiled=True)  37.1 us
    all_to_all x6, waiting for transfers between devices, signal(): lax.all_to_all(imag_part, 'seq', split_axis=2, concat_axis=1, tiled=True)  34.4 us
    all_to_all x5, starting transfers between devices, signal(): lax.all_to_all(columns, 'seq', split_axis=1, concat_axis=2, tiled=True)  34.3 us
    all_to_all x6, waiting for transfers between devices, order_spectrum(): lax.all_to_all(imag_part, 'seq', split_axis=2, concat_axis=1, tiled=True)  33.6 us
  transfers between devices with their start and end apart: 61, of which 52 were waited for; matrix products, arithmetic and copies ran while one was open for 23% of the time, Pallas kernels for 0%

commit v1 on v0

--- a/solution.py
+++ b/solution.py
@@ -140,7 +140,12 @@
     return local_dft(
         (
             lax.all_to_all(real_part, "seq", split_axis=1, concat_axis=2, tiled=True),
-            lax.all_to_all(imag_part, "seq", split_axis=1, concat_axis=2, tiled=True),
+            jnp.concatenate(
+                lax.all_to_all(
+                    jnp.stack(jnp.split(imag_part, lax.axis_size("seq"), axis=1)), "seq", 0, 0
+                ),
+                axis=2,
+            ),
         )
     )
 

time: 1310 us -> 1350 us (1.031)
  local copies, waits for them, and re-layouts: 193 us -> 239 us
  blocking collectives: 118 us -> 93.9 us
  starting transfers between devices: 315 us -> 336 us
    unnamed x186 -> x280, local copies, waits for them, and re-layouts: 50.7 us -> 96.3 us
    all_to_all x2 -> x0, blocking collectives: 24.2 us -> none  [the longest x1 12.2 us: spectrum(): lax.all_to_all(field, 'seq', split_axis=2, concat_axis=1, tiled=True)]
    all_to_all x5 -> x6, starting transfers between devices: 34.3 us -> 39 us  [signal(): lax.all_to_all(columns, 'seq', split_axis=1, concat_axis=2, tiled=True)]
    all_to_all x5 -> x6, starting transfers between devices: 29.4 us -> 33.6 us  [spectrum(): lax.all_to_all(field, 'seq', split_axis=2, concat_axis=1, tiled=True)]
    all_to_all x5 -> x6, waiting for transfers between devices: 28.9 us -> 32.2 us  [signal(): lax.all_to_all(columns, 'seq', split_axis=1, concat_axis=2, tiled=True)]
  transfers between devices with their start and end apart: 61 -> 63, of which waited for: 52 -> 50; matrix products, arithmetic and copies ran while one was open for 23% -> 27% of each run, Pallas kernels for 0% -> 0%
where the time goes in v1:
time: 1350 us; the launch traced here: 1330 us
  waiting for transfers between devices  414 us (31%)
  starting transfers between devices  336 us (25%)
  local copies, waits for them, and re-layouts  239 us (18%)
  matrix products  156 us (12%)
  blocking collectives  93.9 us (7%)
  other arithmetic  75.1 us (6%)
  between operations  16.8 us (1%)
    psum x1, waiting for transfers between devices, shards(): lax.psum((local_w_in, local_w_out, local_taps, local_skip_one, local_skip...  138 us
    unnamed x280, local copies, waits for them, and re-layouts  96.3 us
    psum x1, blocking collectives, shards(): lax.psum((local_w_in, local_w_out, local_taps, local_skip_one, local_skip...  66.5 us
    all_to_all x6, starting transfers between devices, signal(): lax.all_to_all(columns, 'seq', split_axis=1, concat_axis=2, tiled=True)  39 us
    all_to_all x6, waiting for transfers between devices, order_spectrum(): lax.all_to_all(imag_part, 'seq', split_axis=2, concat_axis=1, tiled=True)  38.8 us
    all_to_all x6, waiting for transfers between devices, restore_spectrum(): lax.all_to_all(real_part, 'seq', split_axis=1, concat_axis=2, tiled=True)  35.8 us
    all_to_all x6, starting transfers between devices, to_frequency(): lax.all_to_all(real_part, 'seq', split_axis=1, concat_axis=2, tiled=True)  35.8 us
    all_to_all x6, starting transfers between devices, restore_spectrum(): lax.all_to_all(imag_part, 'seq', split_axis=1, concat_axis=2, tiled=True)  34.5 us
  transfers between devices with their start and end apart: 63, of which 50 were waited for; matrix products, arithmetic and copies ran while one was open for 27% of the time, Pallas kernels for 0%

profile of v1, /device:TPU:1, one launch (start us, length us, event | category | flops | bytes accessed | tf_op | source)
XLA Modules:
  0.0 1330.5 jit_solution(12660615146421666511)
XLA Ops:
  10.7 9.3 all-to-all-start.4
  30.2 6.5 all-to-all-start
  38.8 5.2 all-to-all-done
  52.5 6.0 all-to-all-done.5
  63.8 5.8 all-to-all-done.6
  76.9 5.2 all-to-all-done.8
  100.5 5.9 all-to-all-start.10
  111.1 6.6 all-to-all-done.10
  136.1 5.1 all-to-all-done.12
  148.2 8.3 all-to-all-done.11
  161.7 10.7 all-to-all-done.13
  172.4 5.3 all-to-all-start.2
  195.9 7.3 all-to-all-start.14
  206.2 8.3 all-to-all-done.14
  231.7 7.3 all-to-all-start.1
  247.1 7.8 all-to-all-start.16
  270.9 7.2 all-to-all-start.17
  282.5 7.1 all-to-all-done.17
  300.3 6.2 all-to-all-done.18
  317.0 6.0 all-to-all-done.19
  323.0 5.1 all-to-all-start.30
  347.8 7.3 all-to-all-start.31
  388.6 7.2 all-to-all-start.20
  397.8 9.6 all-to-all-done.20
  417.6 6.4 all-to-all-done.32
  440.6 5.3 all-to-all-start.3
  454.5 7.3 all-to-all-start.23
  478.8 6.3 all-to-all-done.33
  494.4 7.4 all-to-all-done.34
  501.8 5.6 all-to-all-start.24
  511.6 7.2 all-to-all-done.24
  518.8 5.1 all-to-all-start.22
  554.2 10.7 fusion.14
  567.9 7.3 all-to-all-start.26
  578.3 8.3 all-to-all-done.26
  594.7 8.5 all-to-all-done.25
  603.3 5.4 all-to-all-start.36
  630.0 6.0 all-to-all-done.35
  646.7 5.4 all-to-all-start.37
  657.2 6.3 all-to-all-done.37
  663.5 5.1 all-to-all-start.38
  672.7 7.5 all-to-all-done.38
  689.3 7.4 all-to-all-done.28
  707.0 5.7 all-to-all-done.27
  725.8 5.5 all-to-all-done.39
  738.9 5.7 all-to-all-done.29
  770.7 7.3 all-to-all-start.55
  785.4 6.1 all-to-all-start.41
  796.0 6.9 all-to-all-done.41
  802.9 5.1 all-to-all-start.42
  829.6 6.5 all-to-all-start.43
  847.5 5.1 all-to-all-start.44
  872.2 8.3 fusion.12
  911.1 7.4 all-to-all-start.57
  969.8 7.3 all-to-all-start.46
  981.8 6.7 all-to-all-done.46
  995.1 9.3 all-to-all-done.45
  1004.5 5.4 all-to-all-start.59
  1035.6 8.4 all-to-all-done.47
  1051.9 27.3 %all-reduce.2 = (bf16[8,512]{1,0:T(8,128)(2,1)}, bf16[8,512]{1,0:T(8,128)(2,1)}) all-reduce(bf16[8,512]{1,0:T(8,128)(2,1)S(1)} %bitcast.1811, bf16[8,512]{1,0:T(8,128)(2,1)S(1)} %bitcast.1810), channel_id=1, replica_groups=mesh['dp'=8,'seq'=16] {'dp'}, use_global_device_ids=true, to_apply=%region_12.13 | all-reduce | flops 8192 | bytes 32768 | tf_op jit(solution)/shard_map/psum | solution.py:329
  1082.9 14.8 %all-to-all-start.49 = ((f32[1,16,32,128]{3,2,0,1:T(8,128)}), f32[1,16,32,128]{3,2,0,1:T(8,128)S(1)}, u32[]{:S(2)}, u32[]{:S(2)}) async-start(f32[1,16,32,128]{3,2,0,1:T(8,128)} %copy.813), calls=%async_computation.49 | async-start | bytes 524288 | tf_op jit(solution)/shard_map/all_to_all | solution.py:168
  1099.0 7.4 all-to-all-done.49
  1112.3 66.5 %all-reduce = (f32[3,384]{1,0:T(4,128)S(1)}, f32[128]{0:T(128)S(1)}, f32[128]{0:T(128)S(1)}) all-reduce(f32[3,384]{1,0:T(4,128)S(1)} %pad_maximum_fusion.3, f32[128]{0:T(128)S(1)} %copy-done.72, f32[128]{0:T(128)S(1)} %copy-done.71), channel_id=1, replica_groups=mesh['dp'=8,'seq'=16] {'dp','seq'}, use_global_device_ids=true, to_apply=%region_5.6 | all-reduce | flops 1408 | bytes 11264 | tf_op jit(solution)/shard_map/psum | solution.py:325
  1182.4 137.8 %all-reduce.5.cloned.1.call-done = (f32[128,384]{0,1:T(8,128)}, f32[128,128]{1,0:T(8,128)}) async-done(((f32[128,384]{0,1:T(8,128)}, f32[128,128]{1,0:T(8,128)}), (f32[128,384]{0,1:T(8,128)}, f32[128,128]{1,0:T(8,128)})) %all-reduce.5.cloned.1.call-update) | async-done | bytes 262160 | tf_op jit(solution)/shard_map/psum | solution.py:325
  (681 shorter events, 658.3 us)
Async XLA Ops:
  10.7 19.5 %all-to-all-start.4 = ((f32[16,1,256]{2,1,0:T(1,128)}), f32[16,1,256]{2,1,0:T(1,128)S(1)}, u32[]{:S(2)}, u32[]{:S(2)}) async-start(f32[16,1,256]{2,1,0:T(1,128)} %reshape.1199), calls=%async_computation.4 | async-start | bytes 32768 | tf_op jit(solution)/shard_map/all_to_all | solution.py:155
  21.2 8.0 collective-permute-start
  30.2 13.8 %all-to-all-start = ((f32[16,1,256]{2,1,0:T(1,128)}), f32[16,1,256]{2,1,0:T(1,128)S(1)}, u32[]{:S(2)}, u32[]{:S(2)}) async-start(f32[16,1,256]{2,1,0:T(1,128)} %reshape.1209), calls=%async_computation | async-start | bytes 32768 | tf_op jit(solution)/shard_map/all_to_all | solution.py:155
  47.5 11.1 all-to-all-start.5
  58.6 11.1 all-to-all-start.6
  69.6 12.5 all-to-all-start.8
  84.8 15.7 %all-to-all-start.9 = ((f32[1,32,32,128]{3,2,0,1:T(8,128)}), f32[1,32,32,128]{3,2,0,1:T(8,128)S(1)}, u32[]{:S(2)}, u32[]{:S(2)}) async-start(f32[1,32,32,128]{3,2,0,1:T(8,128)} %copy.639), calls=%async_computation.9 | async-start | bytes 1048576 | tf_op jit(solution)/shard_map/all_to_all | solution.py:142
  100.5 17.3 %all-to-all-start.10 = ((f32[16,1,2,32,128]{4,2,3,1,0:T(2,128)}), f32[16,1,2,32,128]{4,2,3,1,0:T(2,128)S(1)}, u32[]{:S(2)}, u32[]{:S(2)}) async-start(f32[16,1,2,32,128]{4,2,3,1,0:T(2,128)} %constant_dynamic-update-slice_fusion.32), calls=%async_computation.10 | async-start | bytes 1048576 | tf_op jit(solution)/shard_map/all_to_all | solution.py:144
  117.7 12.4 all-to-all-start.7
  130.2 11.1 all-to-all-start.12
  141.2 15.2 %all-to-all-start.11 = ((f32[1,2,512,128]{3,1,0,2:T(2,128)}), f32[1,2,512,128]{3,1,0,2:T(2,128)S(1)}, u32[]{:S(2)}, u32[]{:S(2)}) async-start(f32[1,2,512,128]{3,1,0,2:T(2,128)} %copy.648), calls=%async_computation.11 | async-start | bytes 1048576 | tf_op jit(solution)/shard_map/all_to_all | solution.py:177
  156.5 15.9 %all-to-all-start.13 = ((f32[1,2,512,128]{3,1,0,2:T(2,128)}), f32[1,2,512,128]{3,1,0,2:T(2,128)S(1)}, u32[]{:S(2)}, u32[]{:S(2)}) async-start(f32[1,2,512,128]{3,1,0,2:T(2,128)} %copy.659), calls=%async_computation.13 | async-start | bytes 1048576 | tf_op jit(solution)/shard_map/all_to_all | solution.py:178
  172.4 23.5 %all-to-all-start.2 = ((f32[16,1,512]{2,1,0:T(1,128)}), f32[16,1,512]{2,1,0:T(1,128)}, u32[]{:S(2)}, u32[]{:S(2)}) async-start(f32[16,1,512]{2,1,0:T(1,128)} %reshape.1211), calls=%async_computation.2 | async-start | bytes 65536 | tf_op jit(solution)/shard_map/all_to_all | solution.py:144
  195.9 18.7 %all-to-all-start.14 = ((f32[1,32,32,128]{3,2,0,1:T(8,128)}), f32[1,32,32,128]{3,2,0,1:T(8,128)S(1)}, u32[]{:S(2)}, u32[]{:S(2)}) async-start(f32[1,32,32,128]{3,2,0,1:T(8,128)} %copy.663), calls=%async_computation.14 | async-start | bytes 1048576 | tf_op jit(solution)/shard_map/all_to_all | solution.py:187
  214.6 17.1 %all-to-all-start.15 = ((f32[1,32,32,128]{3,2,0,1:T(8,128)}), f32[1,32,32,128]{3,2,0,1:T(8,128)}, u32[]{:S(2)}, u32[]{:S(2)}) async-start(f32[1,32,32,128]{3,2,0,1:T(8,128)} %copy.665), calls=%async_computation.15 | async-start | bytes 1048576 | tf_op jit(solution)/shard_map/all_to_all | solution.py:188
  231.7 15.4 %all-to-all-start.1 = ((f32[16,1,512]{2,1,0:T(1,128)}), f32[16,1,512]{2,1,0:T(1,128)}, u32[]{:S(2)}, u32[]{:S(2)}) async-start(f32[16,1,512]{2,1,0:T(1,128)} %reshape.1213), calls=%async_computation.1 | async-start | bytes 65536 | tf_op jit(solution)/shard_map/all_to_all | solution.py:142
  247.1 23.8 %all-to-all-start.16 = ((f32[1,2,512,128]{3,1,0,2:T(2,128)}), f32[1,2,512,128]{3,1,0,2:T(2,128)}, u32[]{:S(2)}, u32[]{:S(2)}) async-start(f32[1,2,512,128]{3,1,0,2:T(2,128)} %copy.672), calls=%async_computation.16 | async-start | bytes 1048576 | tf_op jit(solution)/shard_map/all_to_all | solution.py:164
  270.9 18.7 %all-to-all-start.17 = ((f32[1,2,512,128]{3,1,0,2:T(2,128)}), f32[1,2,512,128]{3,1,0,2:T(2,128)}, u32[]{:S(2)}, u32[]{:S(2)}) async-start(f32[1,2,512,128]{3,1,0,2:T(2,128)} %copy.678), calls=%async_computation.17 | async-start | bytes 1048576 | tf_op jit(solution)/shard_map/all_to_all | solution.py:165
  293.4 13.2 all-to-all-start.18
  309.5 13.6 %all-to-all-start.19 = ((f32[1,1,512,128]{3,1,0,2:T(1,128)}), f32[1,1,512,128]{3,1,0,2:T(1,128)}, u32[]{:S(2)}, u32[]{:S(2)}) async-start(f32[1,1,512,128]{3,1,0,2:T(1,128)} %bitcast.1703), calls=%async_computation.19 | async-start | bytes 524288 | tf_op jit(solution)/shard_map/all_to_all | solution.py:155
  323.0 18.8 %all-to-all-start.30 = ((f32[1,1,512,128]{3,1,0,2:T(1,128)}), f32[1,1,512,128]{3,1,0,2:T(1,128)}, u32[]{:S(2)}, u32[]{:S(2)}) async-start(f32[1,1,512,128]{3,1,0,2:T(1,128)} %bitcast.1702), calls=%async_computation.30 | async-start | bytes 524288 | tf_op jit(solution)/shard_map/all_to_all | solution.py:155
  347.8 40.8 %all-to-all-start.31 = ((f32[1,32,32,128]{3,2,0,1:T(8,128)}), f32[1,32,32,128]{3,2,0,1:T(8,128)}, u32[]{:S(2)}, u32[]{:S(2)}) async-start(f32[1,32,32,128]{3,2,0,1:T(8,128)} %copy.733), calls=%async_computation.31 | async-start | bytes 1048576 | tf_op jit(solution)/shard_map/all_to_all | solution.py:142
  388.6 18.7 %all-to-all-start.20 = ((f32[1,32,32,128]{3,2,0,1:T(8,128)}), f32[1,32,32,128]{3,2,0,1:T(8,128)}, u32[]{:S(2)}, u32[]{:S(2)}) async-start(f32[1,32,32,128]{3,2,0,1:T(8,128)} %copy.687), calls=%async_computation.20 | async-start | bytes 1048576 | tf_op jit(solution)/shard_map/all_to_all | solution.py:142
  407.4 16.6 %all-to-all-start.32 = ((f32[16,1,2,32,128]{4,2,3,1,0:T(2,128)}), f32[16,1,2,32,128]{4,2,3,1,0:T(2,128)}, u32[]{:S(2)}, u32[]{:S(2)}) async-start(f32[16,1,2,32,128]{4,2,3,1,0:T(2,128)} %constant_dynamic-update-slice_fusion.64), calls=%async_computation.32 | async-start | bytes 1048576 | tf_op jit(solution)/shard_map/all_to_all | solution.py:144
  424.0 16.6 %all-to-all-start.21 = ((f32[16,1,2,32,128]{4,2,3,1,0:T(2,128)}), f32[16,1,2,32,128]{4,2,3,1,0:T(2,128)}, u32[]{:S(2)}, u32[]{:S(2)}) async-start(f32[16,1,2,32,128]{4,2,3,1,0:T(2,128)} %constant_dynamic-update-slice_fusion.48), calls=%async_computation.21 | async-start | bytes 1048576 | tf_op jit(solution)/shard_map/all_to_all | solution.py:144
  440.6 13.8 %all-to-all-start.3 = ((f32[16,1,512]{2,1,0:T(1,128)}), f32[16,1,512]{2,1,0:T(1,128)}, u32[]{:S(2)}, u32[]{:S(2)}) async-start(f32[16,1,512]{2,1,0:T(1,128)} %reshape.1217), calls=%async_computation.3 | async-start | bytes 65536 | tf_op jit(solution)/shard_map/all_to_all | solution.py:177
  454.5 14.7 %all-to-all-start.23 = ((f32[16,1,512]{2,1,0:T(1,128)}), f32[16,1,512]{2,1,0:T(1,128)}, u32[]{:S(2)}, u32[]{:S(2)}) async-start(f32[16,1,512]{2,1,0:T(1,128)} %reshape.1215), calls=%async_computation.23 | async-start | bytes 65536 | tf_op jit(solution)/shard_map/all_to_all | solution.py:178
  469.2 16.0 %all-to-all-start.33 = ((f32[1,2,512,128]{3,1,0,2:T(2,128)}), f32[1,2,512,128]{3,1,0,2:T(2,128)}, u32[]{:S(2)}, u32[]{:S(2)}) async-start(f32[1,2,512,128]{3,1,0,2:T(2,128)} %copy.742), calls=%async_computation.33 | async-start | bytes 1048576 | tf_op jit(solution)/shard_map/all_to_all | solution.py:177
  485.1 16.6 %all-to-all-start.34 = ((f32[1,2,512,128]{3,1,0,2:T(2,128)}), f32[1,2,512,128]{3,1,0,2:T(2,128)}, u32[]{:S(2)}, u32[]{:S(2)}) async-start(f32[1,2,512,128]{3,1,0,2:T(2,128)} %copy.749), calls=%async_computation.34 | async-start | bytes 1048576 | tf_op jit(solution)/shard_map/all_to_all | solution.py:178
  501.8 17.0 %all-to-all-start.24 = ((f32[1,2,512,128]{3,1,0,2:T(2,128)}), f32[1,2,512,128]{3,1,0,2:T(2,128)}, u32[]{:S(2)}, u32[]{:S(2)}) async-start(f32[1,2,512,128]{3,1,0,2:T(2,128)} %copy.707), calls=%async_computation.24 | async-start | bytes 1048576 | tf_op jit(solution)/shard_map/all_to_all | solution.py:178
  518.8 22.5 %all-to-all-start.22 = ((f32[1,2,512,128]{3,1,0,2:T(2,128)}), f32[1,2,512,128]{3,1,0,2:T(2,128)}, u32[]{:S(2)}, u32[]{:S(2)}) async-start(f32[1,2,512,128]{3,1,0,2:T(2,128)} %copy.696), calls=%async_computation.22 | async-start | bytes 1048576 | tf_op jit(solution)/shard_map/all_to_all | solution.py:177
  567.9 18.7 %all-to-all-start.26 = ((f32[1,32,32,128]{3,2,0,1:T(8,128)}), f32[1,32,32,128]{3,2,0,1:T(8,128)S(1)}, u32[]{:S(2)}, u32[]{:S(2)}) async-start(f32[1,32,32,128]{3,2,0,1:T(8,128)} %copy.713), calls=%async_computation.26 | async-start | bytes 1048576 | tf_op jit(solution)/shard_map/all_to_all | solution.py:188
  586.6 16.6 %all-to-all-start.25 = ((f32[1,32,32,128]{3,2,0,1:T(8,128)}), f32[1,32,32,128]{3,2,0,1:T(8,128)}, u32[]{:S(2)}, u32[]{:S(2)}) async-start(f32[1,32,32,128]{3,2,0,1:T(8,128)} %copy.711), calls=%async_computation.25 | async-start | bytes 1048576 | tf_op jit(solution)/shard_map/all_to_all | solution.py:187
  603.3 16.8 %all-to-all-start.36 = ((f32[1,32,32,128]{3,2,0,1:T(8,128)}), f32[1,32,32,128]{3,2,0,1:T(8,128)}, u32[]{:S(2)}, u32[]{:S(2)}) async-start(f32[1,32,32,128]{3,2,0,1:T(8,128)} %copy.755), calls=%async_computation.36 | async-start | bytes 1048576 | tf_op jit(solution)/shard_map/all_to_all | solution.py:188
  620.0 15.9 %all-to-all-start.35 = ((f32[1,32,32,128]{3,2,0,1:T(8,128)}), f32[1,32,32,128]{3,2,0,1:T(8,128)S(1)}, u32[]{:S(2)}, u32[]{:S(2)}) async-start(f32[1,32,32,128]{3,2,0,1:T(8,128)} %copy.753), calls=%async_computation.35 | async-start | bytes 1048576 | tf_op jit(solution)/shard_map/all_to_all | solution.py:187
  646.7 16.8 %all-to-all-start.37 = ((f32[1,2,512,128]{3,1,0,2:T(2,128)}), f32[1,2,512,128]{3,1,0,2:T(2,128)}, u32[]{:S(2)}, u32[]{:S(2)}) async-start(f32[1,2,512,128]{3,1,0,2:T(2,128)} %copy.760), calls=%async_computation.37 | async-start | bytes 1048576 | tf_op jit(solution)/shard_map/all_to_all | solution.py:164
  663.5 16.6 %all-to-all-start.38 = ((f32[1,2,512,128]{3,1,0,2:T(2,128)}), f32[1,2,512,128]{3,1,0,2:T(2,128)}, u32[]{:S(2)}, u32[]{:S(2)}) async-start(f32[1,2,512,128]{3,1,0,2:T(2,128)} %copy.766), calls=%async_computation.38 | async-start | bytes 1048576 | tf_op jit(solution)/shard_map/all_to_all | solution.py:165
  680.1 16.6 %all-to-all-start.28 = ((f32[1,2,512,128]{3,1,0,2:T(2,128)}), f32[1,2,512,128]{3,1,0,2:T(2,128)}, u32[]{:S(2)}, u32[]{:S(2)}) async-start(f32[1,2,512,128]{3,1,0,2:T(2,128)} %copy.724), calls=%async_computation.28 | async-start | bytes 1048576 | tf_op jit(solution)/shard_map/all_to_all | solution.py:165
  696.8 15.9 %all-to-all-start.27 = ((f32[1,2,512,128]{3,1,0,2:T(2,128)}), f32[1,2,512,128]{3,1,0,2:T(2,128)S(1)}, u32[]{:S(2)}, u32[]{:S(2)}) async-start(f32[1,2,512,128]{3,1,0,2:T(2,128)} %copy.718), calls=%async_computation.27 | async-start | bytes 1048576 | tf_op jit(solution)/shard_map/all_to_all | solution.py:164
  717.5 13.8 %all-to-all-start.39 = ((f32[1,16,32,128]{3,2,0,1:T(8,128)}), f32[1,16,32,128]{3,2,0,1:T(8,128)}, u32[]{:S(2)}, u32[]{:S(2)}) async-start(f32[1,16,32,128]{3,2,0,1:T(8,128)} %copy.771), calls=%async_computation.39 | async-start | bytes 524288 | tf_op jit(solution)/shard_map/all_to_all | solution.py:168
  731.3 13.3 all-to-all-start.29
  744.6 12.1 all-to-all-start.56
  756.7 13.9 %all-to-all-start.40 = ((f32[1,1,512,128]{3,1,0,2:T(1,128)}), f32[1,1,512,128]{3,1,0,2:T(1,128)}, u32[]{:S(2)}, u32[]{:S(2)}) async-start(f32[1,1,512,128]{3,1,0,2:T(1,128)} %bitcast.1706), calls=%async_computation.40 | async-start | bytes 524288 | tf_op jit(solution)/shard_map/all_to_all | solution.py:155
  770.7 14.7 %all-to-all-start.55 = ((f32[16,1,512]{2,1,0:T(1,128)}), f32[16,1,512]{2,1,0:T(1,128)}, u32[]{:S(2)}, u32[]{:S(2)}) async-start(f32[16,1,512]{2,1,0:T(1,128)} %reshape.1231), calls=%async_computation.55 | async-start | bytes 65536 | tf_op jit(solution)/shard_map/all_to_all | solution.py:187
  785.4 17.6 %all-to-all-start.41 = ((f32[1,32,32,128]{3,2,0,1:T(8,128)}), f32[1,32,32,128]{3,2,0,1:T(8,128)}, u32[]{:S(2)}, u32[]{:S(2)}) async-start(f32[1,32,32,128]{3,2,0,1:T(8,128)} %copy.775), calls=%async_computation.41 | async-start | bytes 1048576 | tf_op jit(solution)/shard_map/all_to_all | solution.py:142
  802.9 16.6 %all-to-all-start.42 = ((f32[16,1,2,32,128]{4,2,3,1,0:T(2,128)}), f32[16,1,2,32,128]{4,2,3,1,0:T(2,128)}, u32[]{:S(2)}, u32[]{:S(2)}) async-start(f32[16,1,2,32,128]{4,2,3,1,0:T(2,128)} %constant_dynamic-update-slice_fusion.80), calls=%async_computation.42 | async-start | bytes 1048576 | tf_op jit(solution)/shard_map/all_to_all | solution.py:144
  829.6 18.0 %all-to-all-start.43 = ((f32[1,2,512,128]{3,1,0,2:T(2,128)}), f32[1,2,512,128]{3,1,0,2:T(2,128)}, u32[]{:S(2)}, u32[]{:S(2)}) async-start(f32[1,2,512,128]{3,1,0,2:T(2,128)} %copy.784), calls=%async_computation.43 | async-start | bytes 1048576 | tf_op jit(solution)/shard_map/all_to_all | solution.py:177
  847.5 16.6 %all-to-all-start.44 = ((f32[1,2,512,128]{3,1,0,2:T(2,128)}), f32[1,2,512,128]{3,1,0,2:T(2,128)}, u32[]{:S(2)}, u32[]{:S(2)}) async-start(f32[1,2,512,128]{3,1,0,2:T(2,128)} %copy.791), calls=%async_computation.44 | async-start | bytes 1048576 | tf_op jit(solution)/shard_map/all_to_all | solution.py:178
  886.6 12.4 all-to-all-start.50
  899.0 12.1 all-to-all-start.51
  911.1 14.6 %all-to-all-start.57 = ((f32[16,1,512]{2,1,0:T(1,128)}), f32[16,1,512]{2,1,0:T(1,128)S(1)}, u32[]{:S(2)}, u32[]{:S(2)}) async-start(f32[16,1,512]{2,1,0:T(1,128)} %reshape.1235), calls=%async_computation.57 | async-start | bytes 65536 | tf_op jit(solution)/shard_map/all_to_all | solution.py:164
  925.8 11.1 all-to-all-start.58
  936.8 11.1 all-to-all-start.53
  947.9 22.0 %all-to-all-start.52 = ((f32[16,1,512]{2,1,0:T(1,128)}), f32[16,1,512]{2,1,0:T(1,128)}, u32[]{:S(2)}, u32[]{:S(2)}) async-start(f32[16,1,512]{2,1,0:T(1,128)} %reshape.1225), calls=%async_computation.52 | async-start | bytes 65536 | tf_op jit(solution)/shard_map/all_to_all | solution.py:164
  969.8 18.7 %all-to-all-start.46 = ((f32[1,32,32,128]{3,2,0,1:T(8,128)}), f32[1,32,32,128]{3,2,0,1:T(8,128)S(1)}, u32[]{:S(2)}, u32[]{:S(2)}) async-start(f32[1,32,32,128]{3,2,0,1:T(8,128)} %copy.797), calls=%async_computation.46 | async-start | bytes 1048576 | tf_op jit(solution)/shard_map/all_to_all | solution.py:188
  988.5 15.9 %all-to-all-start.45 = ((f32[1,32,32,128]{3,2,0,1:T(8,128)}), f32[1,32,32,128]{3,2,0,1:T(8,128)S(1)}, u32[]{:S(2)}, u32[]{:S(2)}) async-start(f32[1,32,32,128]{3,2,0,1:T(8,128)} %copy.795), calls=%async_computation.45 | async-start | bytes 1048576 | tf_op jit(solution)/shard_map/all_to_all | solution.py:187
  1004.5 12.4 all-to-all-start.59
  1016.9 11.7 all-to-all-start.54
  1028.6 15.4 %all-to-all-start.47 = ((f32[1,2,512,128]{3,1,0,2:T(2,128)}), f32[1,2,512,128]{3,1,0,2:T(2,128)S(1)}, u32[]{:S(2)}, u32[]{:S(2)}) async-start(f32[1,2,512,128]{3,1,0,2:T(2,128)} %copy.802), calls=%async_computation.47 | async-start | bytes 1048576 | tf_op jit(solution)/shard_map/all_to_all | solution.py:164
  1044.0 35.3 %all-to-all-start.48 = ((f32[1,2,512,128]{3,1,0,2:T(2,128)}), f32[1,2,512,128]{3,1,0,2:T(2,128)S(1)}, u32[]{:S(2)}, u32[]{:S(2)}) async-start(f32[1,2,512,128]{3,1,0,2:T(2,128)} %copy.808), calls=%async_computation.48 | async-start | bytes 1048576 | tf_op jit(solution)/shard_map/all_to_all | solution.py:165
  1082.9 23.5 %all-to-all-start.49 = ((f32[1,16,32,128]{3,2,0,1:T(8,128)}), f32[1,16,32,128]{3,2,0,1:T(8,128)S(1)}, u32[]{:S(2)}, u32[]{:S(2)}) async-start(f32[1,16,32,128]{3,2,0,1:T(8,128)} %copy.813), calls=%async_computation.49 | async-start | bytes 524288 | tf_op jit(solution)/shard_map/all_to_all | solution.py:168
  1097.7 222.5 %all-reduce.5.cloned.1.call-start = ((), (), s32[]{:S(2)}) async-start(), calls=%async_computation.60 | async-start | bytes 524288 | tf_op jit(solution)/shard_map/psum | solution.py:325
  1106.6 4.9 collective-permute-start.1
  1111.6 69.9 %copy-start.46 = (bf16[128,384]{1,0:T(8,128)(2,1)S(1)}, bf16[128,384]{1,0:T(8,128)(2,1)}, u32[]{:S(2)}) copy-start(bf16[128,384]{1,0:T(8,128)(2,1)} %param.11) | copy-start | bytes 294916
  (72 other events, 602.5 us)
Sparse Core Ops, SparseCore 0:
  1181.6 138.5 all-reduce.4
